TPU v7x, 32 devices: a whole 2x2x4 slice. The times are simulated.
32 devices in a mesh: shot: 2 (over x), tile: 16 (over z, y, core).
Axes of the slice: x: 2, y: 2, z: 4, core: 2. Of those that a mesh axis runs over, the one named last changes fastest.
Arguments:
- wave_now: float32 [4, 32, 32, 128], P('shot', 'tile'), parts along dimension 0, may hold values from -6 to 6
- wave_prev: float32 [4, 32, 32, 128], P('shot', 'tile'), parts along dimension 0, may hold values from -6 to 6
- facies: int32 [32, 32, 128], P('tile'), may hold values from 0 to 7
- velocity_table: float32 [8], replicated, may hold values from 0.05 to 0.2
- epsilon_table: float32 [8], replicated, may hold values from 0 to 0.2
- tilt_table: float32 [8], replicated, may hold values from -0.6 to 0.6
- source_cell: int32 [2], P('shot'), parts along dimension 0, may hold values from 0 to 4095
- source_wavelet: float32 [8], P('shot'), parts along dimension 0, may hold values from -8 to 8
- receiver_cells: int32 [4096], P('shot'), parts along dimension 0, may hold values from 0 to 4095
- receiver_data: float32 [4, 4096], P(None, 'shot'), parts along dimension 1, may hold values from -6 to 6
Outputs:
- filtered: bfloat16 [64, 32, 32, 128], P('shot', None, 'tile'), parts along dimension 0
- wave_out: float32 [4, 32, 32, 128], P('shot', 'tile'), parts along dimension 0
There are 2 independent parts, one for each index of `shot`. A program takes and returns all parts, laid end to end along the dimension named above; an argument that names none is the same for every part. Nothing has to cross between parts.
Inputs may be any that keep to these rules, and one draw needn't show every extreme that they name: `source_cell`: a surface cell y * 128 + x. `receiver_cells`: surface cells y * 128 + x; cells may repeat.
All inputs are finite; a program needn't handle non-finite values.
Results may differ from a plain program's by a relative error of at most 0.001.
The roundings to bfloat16 on the way count: a program that leaves them out, or rounds other values in their place, can miss the bound.
Values may be sent and summed in bfloat16 or wider, within the bound.
A program may use at most 64 MiB of HBM per device.

v0:
```python
import functools

import jax
import jax.numpy as jnp
from jax import lax
from jax.experimental import pallas as pl
from jax.experimental.pallas import tpu as pltpu
from jax.sharding import PartitionSpec as P

NLAG = 32
STEPS = 4
HALO = 2
UNROLL = 4
REACH = 4
PARTS = 4


def in_order(count, body):
    def run(i, carry):
        body(i)
        return carry

    lax.fori_loop(0, count, run, 0)


def kernel(
    tiles,
    now,
    prev_in,
    facies_in,
    vel_in,
    eps_in,
    tilt_in,
    src_in,
    wavelet_in,
    cells_in,
    data_in,
    out,
    wave_out,
    prev,
    facies,
    vel_tab,
    eps_tab,
    tilt_tab,
    src_cell,
    wavelet,
    cells,
    data,
    ext0,
    ext1,
    mid0,
    mid1,
    prev_halo,
    fac_halo,
    coef,
    lhs,
    surf,
    turned,
    send,
    recv,
    planes,
    part_image,
    staged,
    woven,
    halo_send,
    halo_recv,
    snap_send,
    snap_recv,
    load_sem,
    near_sem,
):
    rows, depth, cols = facies.shape
    per = depth // tiles
    nrec = data.shape[1]
    ext_rows = rows + 2
    group = 2 * rows
    block = (per + 2) * group
    margin = NLAG // 2
    me = lax.axis_index("tile")
    has_up = me > 0
    has_down = me < tiles - 1

    barrier = pltpu.get_barrier_semaphore()

    def signal_at(semaphore, step):
        for way in (-step, step):
            peer = me + way
            there = (peer >= 0) & (peer < tiles)

            @pl.when(there)
            def _():
                pl.semaphore_signal(semaphore, inc=1, device_id={"tile": peer})

    def wait_at(semaphore, step):
        lower = (me >= step).astype(jnp.int32)
        pl.semaphore_wait(semaphore, lower + (me + step < tiles).astype(jnp.int32))

    near = range(1, min(REACH, tiles - 1) + 1)
    for step in near:
        signal_at(barrier, step)

    reaches = []
    while (REACH << len(reaches)) < tiles - 1:
        reaches.append(REACH << len(reaches))

    loads = [
        pltpu.make_async_copy(src, dst, load_sem.at[n])
        for n, (src, dst) in enumerate(
            (
                (cells_in, cells),
                (data_in, data),
                (facies_in, facies),
                (vel_in, vel_tab),
                (eps_in, eps_tab),
                (tilt_in, tilt_tab),
                (src_in, src_cell),
                (wavelet_in, wavelet),
                (now, ext0.at[:, HALO : HALO + rows]),
                (prev_in, prev),
            )
        )
    ]
    for load in loads:
        load.start()
    zero_plane = jnp.zeros((depth, cols), jnp.float32)
    def clear_side(side, row):
        for f in range(2):
            for i in range(HALO):
                ext0[f, row + i] = zero_plane
                ext1[f, row + i] = zero_plane
            prev_halo[side, f] = zero_plane
        fac_halo[side] = jnp.full((depth, cols), -1, jnp.int32)

    @pl.when(jnp.logical_not(has_up))
    def _():
        clear_side(0, 0)

    @pl.when(jnp.logical_not(has_down))
    def _():
        clear_side(1, rows + HALO)

    reach = min(REACH, tiles - 1)
    pl.semaphore_wait(barrier, jnp.minimum(me, reach) + jnp.minimum(tiles - 1 - me, reach))

    def remote(src, dst, ssem, rsem, peer):
        return pltpu.make_async_remote_copy(
            src_ref=src, dst_ref=dst, send_sem=ssem, recv_sem=rsem, device_id={"tile": peer}
        )

    def halo_copies(side):
        peer = me - 1 if side == 0 else me + 1
        first = 0 if side == 0 else rows - HALO
        edge = 0 if side == 0 else rows - 1
        other = 1 - side
        into = rows + HALO if side == 0 else 0
        sems = lambda n: (halo_send.at[side, n], halo_recv.at[other, n], peer)
        return (
            remote(now.at[:, first : first + HALO], ext0.at[:, into : into + HALO], *sems(0)),
            remote(facies_in.at[edge], fac_halo.at[other], *sems(1)),
            remote(prev_in.at[:, edge], prev_halo.at[other], *sems(2)),
        )

    def wave_copy(side):
        peer = me - 1 if side == 0 else me + 1
        first = HALO if side == 0 else rows
        into = rows + HALO if side == 0 else 0
        return remote(
            ext1.at[:, first : first + HALO], ext1.at[:, into : into + HALO],
            halo_send.at[side, 3], halo_recv.at[1 - side, 3], peer,
        )

    def arrivals(side, count):
        into = 0 if side == 0 else rows + HALO
        peer = me
        sems = lambda n: (halo_send.at[side, n], halo_recv.at[side, n], peer)
        if count == 3:
            return (
                remote(now.at[:, 0:HALO], ext0.at[:, into : into + HALO], *sems(0)),
                remote(facies_in.at[0], fac_halo.at[side], *sems(1)),
                remote(prev_in.at[:, 0], prev_halo.at[side], *sems(2)),
            )
        return (remote(ext1.at[:, HALO : 2 * HALO], ext1.at[:, into : into + HALO], *sems(3)),)

    def each_side(action):
        for side, there in ((0, has_up), (1, has_down)):
            @pl.when(there)
            def _():
                action(side)

    def start_halo(side):
        for copy in halo_copies(side):
            copy.start()

    def wait_halo(side):
        for copy in arrivals(side, 3):
            copy.wait_recv()

    def wait_wave(side):
        for copy in arrivals(side, 1):
            copy.wait_recv()

    if reaches:
        signal_at(near_sem.at[0], reaches[0])
    each_side(start_halo)

    for load in loads[:2]:
        load.wait()

    cell = cells[...]
    column = cell & (cols - 1) if cols & (cols - 1) == 0 else lax.rem(cell, cols)
    onehot = (lax.broadcasted_iota(jnp.int32, (cols, nrec), 0) == column).astype(jnp.float32)
    onehot = onehot.astype(jnp.bfloat16)
    amounts = data[...]
    high = amounts.astype(jnp.bfloat16).astype(jnp.float32)
    rest = amounts - high
    middle = rest.astype(jnp.bfloat16).astype(jnp.float32)
    parts = (high, middle, rest - middle, jnp.zeros_like(high))
    for i in range(ext_rows):
        first = (me * rows + i - 1) * cols
        inside = (cell >= first) & (cell < first + cols)
        for p, part in enumerate(parts):
            at = (i * PARTS + p) * STEPS
            lhs[at : at + STEPS, :] = jnp.where(inside, part, 0.0)
    surf[...] = lax.dot_general(
        lhs[...].astype(jnp.bfloat16), onehot, (((1,), (1,)), ((), ())),
        preferred_element_type=jnp.float32,
    )

    def fill_coef(i, kinds):
        vel = jnp.zeros((depth, cols), jnp.float32)
        eps, tlt = vel, vel
        for n in range(vel_tab.shape[0]):
            here = kinds == n
            vel = jnp.where(here, vel_tab[n], vel)
            eps = jnp.where(here, eps_tab[n], eps)
            tlt = jnp.where(here, tilt_tab[n], tlt)
        coef[0, i] = vel
        coef[1, i] = 1.0 + 2.0 * eps
        coef[2, i] = 0.25 * tlt

    for load in loads[2:]:
        load.wait()
    for i in range(rows):
        fill_coef(i + 1, facies[i])
    turned[0:group, :] = jnp.zeros((group, cols), jnp.float32)
    turned[group * (depth + 1) : group * (depth + 2), :] = jnp.zeros((group, cols), jnp.float32)

    each_side(wait_halo)
    if reaches:
        wait_at(near_sem.at[0], reaches[0])
    if len(reaches) > 1:
        signal_at(near_sem.at[1], reaches[1])
    fill_coef(0, fac_halo[0])
    fill_coef(rows + 1, fac_halo[1])

    lane = lax.broadcasted_iota(jnp.int32, (depth, cols), 1)
    level = lax.broadcasted_iota(jnp.int32, (depth, cols), 0)
    first_lane, last_lane = lane == 0, lane == cols - 1
    first_level, last_level = level == 0, level == depth - 1
    surface_lane = lax.broadcasted_iota(jnp.int32, (1, cols), 1)

    def advance(step, f, i, current, above, below, old):
        right = lambda v: jnp.where(last_lane, 0.0, pltpu.roll(v, cols - 1, 1))
        left = lambda v: jnp.where(first_lane, 0.0, pltpu.roll(v, 1, 1))
        deeper = jnp.where(last_level, 0.0, pltpu.roll(current, depth - 1, 0))
        higher = jnp.where(first_level, 0.0, pltpu.roll(current, 1, 0))
        twice = 2.0 * current
        along_x = right(current) + left(current) - twice
        along_y = above + below - twice
        along_z = deeper + higher - twice
        slope = deeper - higher
        mixed = right(slope) - left(slope)
        operator = coef[1, i] * (along_x + along_y) + along_z + coef[2, i] * mixed
        new = twice - old + coef[0, i] * operator
        if f == 0:
            target = src_cell[0] - (me * rows + i - 1) * cols
            added = jnp.where(surface_lane == target, wavelet[step], 0.0)
        else:
            at = i * PARTS * STEPS + step
            added = surf[at : at + 1, :]
            for p in range(1, 3):
                added = added + surf[at + p * STEPS : at + p * STEPS + 1, :]
        return new + jnp.where(first_level, added, 0.0)

    def outer_step(step, ext, before, into):
        for f in range(2):
            for i in range(ext_rows):
                into[f, i] = advance(
                    step, f, i, ext[f, i + 1], ext[f, i], ext[f, i + 2], before(f, i)
                )

    def inner_step(step, mid, before, store):
        for f in range(2):
            for i in range(rows):
                new = advance(
                    step, f, i + 1, mid[f, i + 1], mid[f, i], mid[f, i + 2], before[f, i + HALO]
                )
                store(f, i, new)
                turned[pl.ds(group + f * rows + i, depth, stride=group), :] = new

    def prev_row(f, i):
        if i == 0:
            return prev_halo[0, f]
        if i == rows + 1:
            return prev_halo[1, f]
        return prev[f, i - 1]

    def pack_snapshot(s):
        for d in range(tiles):
            at = d * per * group
            send[s, d] = turned[at : at + block, :].astype(jnp.bfloat16)

    def snap_copy(s, peer):
        return remote(
            send.at[s, peer], recv.at[s, me], snap_send.at[s, peer], snap_recv.at[s, me], peer
        )

    def send_snapshot(s):
        in_order(tiles - 1, lambda i: snap_copy(s, lax.rem(me + 1 + i, tiles)).start())
        recv[s, me] = send[s, me]

    def await_snapshot(s):
        def body(i):
            peer = lax.rem(me + 1 + i, tiles)
            remote(
                send.at[s, me], recv.at[s, peer], snap_send.at[s, me], snap_recv.at[s, peer], peer
            ).wait_recv()

        in_order(tiles - 1, body)

    def open_snapshot(s):
        staged[...] = recv[s].reshape(tiles * block, cols).astype(jnp.float32)
        for f in range(2):
            for j in range(per + 2):
                for r in range(rows):
                    at = (j * rows + r) * tiles
                    planes[s, f, at : at + tiles, :] = staged[
                        pl.ds(j * group + f * rows + r, tiles, stride=block), :
                    ]

    outer_step(0, ext0, prev_row, mid0)

    def keep_ext1(f, i, new):
        ext1[f, i + HALO] = new

    inner_step(1, mid0, ext0, keep_ext1)
    each_side(lambda side: wave_copy(side).start())
    pack_snapshot(0)
    for n in range(1, len(reaches)):
        wait_at(near_sem.at[n], reaches[n])
        if n + 1 < len(reaches):
            signal_at(near_sem.at[n + 1], reaches[n + 1])
    send_snapshot(0)
    each_side(wait_wave)
    outer_step(2, ext1, lambda f, i: mid0[f, i], mid1)

    def keep_out(f, i, new):
        wave_out[f, i] = new

    inner_step(3, mid1, ext1, keep_out)
    pack_snapshot(1)
    send_snapshot(1)

    await_snapshot(0)
    open_snapshot(0)

    def pulled(s, k):
        shift = lax.rem(2 * margin - 2 * k + 2 * cols, cols)
        return planes[s, 0] * pltpu.roll(planes[s, 1], shift, 1)

    def first_products(k):
        part_image[k] = pulled(0, k)

    in_order(NLAG, first_products)
    await_snapshot(1)
    open_snapshot(1)

    image_rows = (per + 2) * rows * tiles
    plane_rows = rows * tiles
    image_lane = lax.broadcasted_iota(jnp.int32, (1, cols), 1)
    tile_index = lax.broadcasted_iota(jnp.int32, (tiles, cols), 0)

    def finish(u, k):
        h = k - margin
        far = image_lane + 2 * h
        valid = (far >= 0) & (far < cols)
        image = jnp.where(valid, part_image[k] + pulled(1, k), 0.0)
        image = image.astype(jnp.bfloat16).astype(jnp.float32)
        own = image[plane_rows : plane_rows * (per + 1)]
        at_first = image_lane == lax.rem(cols - h, cols)
        at_last = image_lane == lax.rem(2 * cols - 1 - h, cols)
        total = jnp.where(at_first, 0.0, pltpu.roll(own, 1, 1))
        total = total + jnp.where(at_last, 0.0, pltpu.roll(own, cols - 1, 1))
        total = total + image[: plane_rows * per] + image[2 * plane_rows :]
        pieces = []
        for z in range(per):
            for r in range(rows):
                here = lambda q: own[z * plane_rows + q * tiles : z * plane_rows + (q + 1) * tiles]
                if r > 0:
                    low = here(r - 1)
                else:
                    low = jnp.where(tile_index == 0, 0.0, pltpu.roll(here(rows - 1), 1, 0))
                if r < rows - 1:
                    high = here(r + 1)
                else:
                    high = jnp.where(
                        tile_index == tiles - 1, 0.0, pltpu.roll(here(0), tiles - 1, 0)
                    )
                pieces.append(low + high)
        total = total + jnp.concatenate(pieces, axis=0)
        result = 0.125 * (6.0 * own - total)
        result = pltpu.roll(result, lax.rem(h + cols, cols), 1)
        for z in range(per):
            for r in range(rows):
                at = z * plane_rows + r * tiles
                woven[u, pl.ds(r * per + z, tiles, stride=rows * per), :] = result[at : at + tiles]
        out[k] = woven[u].astype(jnp.bfloat16)

    def finish_some(b):
        for u in range(UNROLL):
            finish(u, b * UNROLL + u)

    in_order(NLAG // UNROLL, finish_some)

    def sent(side):
        for copy in halo_copies(side):
            copy.wait_send()
        wave_copy(side).wait_send()

    each_side(sent)
    for s in range(2):
        in_order(tiles - 1, lambda i: snap_copy(s, lax.rem(me + 1 + i, tiles)).wait_send())


def shards(tiles, now, prev, facies, vel, eps, tilt, src_cell, wavelet, cells, data):
    rows, depth, cols = facies.shape
    per = depth // tiles
    nrec = cells.shape[0]
    block = (per + 2) * 2 * rows
    image_rows = (per + 2) * rows * tiles
    f32 = jnp.float32
    vmem = pl.BlockSpec(memory_space=pltpu.VMEM)
    hbm = pl.BlockSpec(memory_space=pltpu.HBM)
    lhs_rows = (rows + 2) * PARTS * STEPS
    filtered, wave = pl.pallas_call(
        functools.partial(kernel, tiles),
        out_shape=(
            pltpu.VMEM((NLAG, rows * tiles * per, cols), jnp.bfloat16),
            pltpu.VMEM(now.shape, f32),
        ),
        in_specs=[hbm] * 10,
        out_specs=(vmem, vmem),
        scratch_shapes=[
            pltpu.VMEM(prev.shape, f32),
            pltpu.VMEM(facies.shape, jnp.int32),
            pltpu.SMEM(vel.shape, f32),
            pltpu.SMEM(eps.shape, f32),
            pltpu.SMEM(tilt.shape, f32),
            pltpu.SMEM(src_cell.shape, jnp.int32),
            pltpu.SMEM(wavelet.shape, f32),
            pltpu.VMEM((1, nrec), jnp.int32),
            pltpu.VMEM(data.shape, f32),
            pltpu.VMEM((2, rows + 2 * HALO, depth, cols), f32),
            pltpu.VMEM((2, rows + 2 * HALO, depth, cols), f32),
            pltpu.VMEM((2, rows + 2, depth, cols), f32),
            pltpu.VMEM((2, rows + 2, depth, cols), f32),
            pltpu.VMEM((2, 2, depth, cols), f32),
            pltpu.VMEM((2, depth, cols), jnp.int32),
            pltpu.VMEM((3, rows + 2, depth, cols), f32),
            pltpu.VMEM((lhs_rows, nrec), f32),
            pltpu.VMEM((lhs_rows, cols), f32),
            pltpu.VMEM((2 * rows * (depth + 2), cols), f32),
            pltpu.VMEM((2, tiles, block, cols), jnp.bfloat16),
            pltpu.VMEM((2, tiles, block, cols), jnp.bfloat16),
            pltpu.VMEM((2, 2, image_rows, cols), f32),
            pltpu.VMEM((NLAG, image_rows, cols), f32),
            pltpu.VMEM((tiles * block, cols), f32),
            pltpu.VMEM((UNROLL, rows * tiles * per, cols), f32),
            pltpu.SemaphoreType.DMA((2, 4)),
            pltpu.SemaphoreType.DMA((2, 4)),
            pltpu.SemaphoreType.DMA((2, tiles)),
            pltpu.SemaphoreType.DMA((2, tiles)),
            pltpu.SemaphoreType.DMA((10,)),
            pltpu.SemaphoreType.REGULAR((max(1, tiles.bit_length()),)),
        ],
        compiler_params=pltpu.CompilerParams(collective_id=0, has_side_effects=True),
    )(now, prev, facies, vel, eps, tilt, src_cell, wavelet, cells.reshape(1, nrec), data)
    return filtered.reshape(NLAG, rows * tiles, per, cols), wave


def solution(mesh):
    return jax.shard_map(
        functools.partial(shards, mesh.shape["tile"]),
        mesh=mesh,
        in_specs=(
            P("shot", "tile", None, None),
            P("shot", "tile", None, None),
            P("tile", None, None),
            P(),
            P(),
            P(),
            P("shot"),
            P("shot"),
            P("shot"),
            P(None, "shot"),
        ),
        out_specs=(P("shot", None, "tile", None), P("shot", "tile", None, None)),
        check_vma=False,
    )
```

profile of v0, /device:TPU:0, one launch (start us, length us, event | category | flops | bytes accessed | tf_op | source)
XLA Modules:
  0.0 23.2 jit_solution(10599418880821536938)
XLA Ops:
  1.3 20.5 %shard_map.113 = (bf16[32,64,128]{2,1,0:T(8,128)(2,1)S(1)}, f32[2,2,32,128]{3,2,1,0:T(8,128)S(1)}) custom-call(f32[2,2,32,128]{3,2,1,0:T(8,128)} %now.1, f32[2,2,32,128]{3,2,1,0:T(8,128)} %prev_in.1, s32[2,32,128]{2,1,0:T(8,128)} %facies_in.1, f32[8]{0:T(128)} %vel_in.1, f32[8]{0:T(128)} %eps_in.1, f32[8]{0:T(128)} %tilt_in.1, s32[1]{0:T(128)S(6)} %copy.16.src_in, ...), custom_call_target="tpu_custom_call" | custom-call | tf_op jit(solution)/shard_map/pallas_call | solution.py:445
  21.8 0.8 %copy.14 = bf16[32,32,2,128]{3,2,1,0:T(2,128)(2,1)} copy(bf16[32,32,2,128]{3,2,1,0:T(2,128)(2,1)S(1)} %bitcast.2) | data formatting | bytes 1048576
  22.6 0.6 %copy.15 = f32[2,2,32,128]{3,2,1,0:T(8,128)} copy(f32[2,2,32,128]{3,2,1,0:T(8,128)S(1)} %get-tuple-element.7) | data formatting | bytes 131072
where the time goes:
time: 23.4 us; the launch traced here: 23.2 us
  Pallas kernels  20.5 us (88%)
  local copies, waits for them, and re-layouts  1.42 us (6%)
  between operations  1.29 us (6%)
    pallas_call x1, Pallas kernels, shards(): pl.pallas_call(functools.partial(kernel, tiles), out_shape=(pltpu.VMEM((N...  20.5 us
    unnamed x2, local copies, waits for them, and re-layouts  1.42 us

commit v1 on v0

v1 whole, which is shorter than its diff:
```python
import functools

import jax
import jax.numpy as jnp
from jax import lax
from jax.experimental import pallas as pl
from jax.experimental.pallas import tpu as pltpu
from jax.sharding import PartitionSpec as P

NLAG = 32
STEPS = 4
REACH = 4
PARTS = 4
LINES = 8


def in_order(count, body):
    def run(i, carry):
        body(i)
        return carry

    lax.fori_loop(0, count, run, 0)


def kernel(
    tiles,
    now,
    prev_in,
    facies_in,
    vel_in,
    eps_in,
    tilt_in,
    src_in,
    wavelet_in,
    cells_in,
    data_in,
    out,
    wave_out,
    own,
    prev,
    facies,
    vel_tab,
    eps_tab,
    tilt_tab,
    src_cell,
    wavelet,
    cells,
    data,
    mate_now,
    mate_prev,
    mate_fac,
    mate_two,
    trace_send,
    trace_recv,
    fac_send,
    fac_recv,
    two,
    work,
    coef,
    far_two,
    lhs,
    surf,
    blocks,
    send,
    recv,
    staged,
    part_image,
    last_own,
    last_sum,
    woven,
    mate_send_sem,
    mate_recv_sem,
    far_send_sem,
    far_recv_sem,
    snap_send,
    snap_recv,
    load_sem,
    near_sem,
):
    rows, depth, cols = facies.shape
    per = depth // tiles
    nrec = data.shape[1]
    group = 2 * rows * (per + 2)
    margin = NLAG // 2
    ngroups = tiles * rows // LINES
    members = LINES // rows
    pairs = (per + 2) // 2
    me = lax.axis_index("tile")
    odd = lax.rem(me, 2)
    even = 1 - odd
    mate = me + 1 - 2 * odd
    far = me - 1 + 2 * odd
    has_far = (far >= 0) & (far < tiles)

    barrier = pltpu.get_barrier_semaphore()

    def signal_at(semaphore, step):
        for way in (-step, step):
            peer = me + way
            there = (peer >= 0) & (peer < tiles)

            @pl.when(there)
            def _():
                pl.semaphore_signal(semaphore, inc=1, device_id={"tile": peer})

    def wait_at(semaphore, step):
        lower = (me >= step).astype(jnp.int32)
        pl.semaphore_wait(semaphore, lower + (me + step < tiles).astype(jnp.int32))

    for step in range(1, min(REACH, tiles - 1) + 1):
        signal_at(barrier, step)

    reaches = []
    while (REACH << len(reaches)) < tiles - 1:
        reaches.append(REACH << len(reaches))

    loads = [
        pltpu.make_async_copy(src, dst, load_sem.at[n])
        for n, (src, dst) in enumerate(
            (
                (cells_in, cells),
                (data_in, data),
                (facies_in, facies),
                (vel_in, vel_tab),
                (eps_in, eps_tab),
                (tilt_in, tilt_tab),
                (src_in, src_cell),
                (wavelet_in, wavelet),
                (now, own),
                (prev_in, prev),
            )
        )
    ]
    for load in loads:
        load.start()
    zero_plane = jnp.zeros((depth, cols), jnp.float32)

    @pl.when(jnp.logical_not(has_far))
    def _():
        for f in range(2):
            for k in range(STEPS):
                trace_recv[k, f] = zero_plane
        for n in range(2):
            fac_recv[n] = jnp.full((depth, cols), -1.0, jnp.bfloat16)

    def remote(src, dst, ssem, rsem, peer):
        return pltpu.make_async_remote_copy(
            src_ref=src, dst_ref=dst, send_sem=ssem, recv_sem=rsem, device_id={"tile": peer}
        )

    def mate_copy(n, src, dst):
        return remote(src, dst, mate_send_sem.at[n], mate_recv_sem.at[n], mate)

    def far_copy(n, src, dst):
        return remote(src, dst, far_send_sem.at[n], far_recv_sem.at[n], far)

    mate_first = (
        mate_copy(0, own, mate_now),
        mate_copy(1, prev.at[:, even], mate_prev),
        mate_copy(2, facies.at[even], mate_fac),
    )
    mate_second = mate_copy(3, two, mate_two)
    far_first = (
        far_copy(0, fac_send, fac_recv),
        far_copy(1, own.at[:, odd], trace_recv.at[0]),
        far_copy(2, trace_send.at[0], trace_recv.at[1]),
    )
    far_second = far_copy(3, trace_send.at[1:3], trace_recv.at[2:4])

    lines = (me * rows + odd, me * rows + even, mate * rows + odd)

    for load in loads[:2]:
        load.wait()

    cell = cells[...]
    column = cell & (cols - 1) if cols & (cols - 1) == 0 else lax.rem(cell, cols)
    onehot = (lax.broadcasted_iota(jnp.int32, (cols, nrec), 0) == column).astype(jnp.float32)
    onehot = onehot.astype(jnp.bfloat16)
    amounts = data[...]
    high = amounts.astype(jnp.bfloat16).astype(jnp.float32)
    rest = amounts - high
    middle = rest.astype(jnp.bfloat16).astype(jnp.float32)
    parts = (high, middle, rest - middle, jnp.zeros_like(high))
    for i in range(3):
        first = lines[i] * cols
        inside = (cell >= first) & (cell < first + cols)
        for p, part in enumerate(parts):
            at = (i * PARTS + p) * STEPS
            lhs[at : at + STEPS, :] = jnp.where(inside, part, 0.0)
    surf[...] = lax.dot_general(
        lhs[...].astype(jnp.bfloat16), onehot, (((1,), (1,)), ((), ())),
        preferred_element_type=jnp.float32,
    )

    def looked_up(kinds):
        vel = jnp.zeros((depth, cols), jnp.float32)
        eps, tlt = vel, vel
        for n in range(vel_tab.shape[0]):
            here = kinds == n
            vel = jnp.where(here, vel_tab[n], vel)
            eps = jnp.where(here, eps_tab[n], eps)
            tlt = jnp.where(here, tilt_tab[n], tlt)
        return vel, vel * (1.0 + 2.0 * eps), 0.25 * vel * tlt

    def fill_coef(i, kinds):
        vel, flat, tlt = looked_up(kinds)
        coef[0, i] = 2.0 - 4.0 * flat - 2.0 * vel
        coef[1, i] = flat
        coef[2, i] = vel
        coef[3, i] = tlt

    lane = lax.broadcasted_iota(jnp.int32, (depth, cols), 1)
    level = lax.broadcasted_iota(jnp.int32, (depth, cols), 0)
    first_lane, last_lane = lane == 0, lane == cols - 1
    first_level, last_level = level == 0, level == depth - 1
    surface_lane = lax.broadcasted_iota(jnp.int32, (1, cols), 1)

    def advance(i, current, above, below, old):
        right = lambda v: jnp.where(last_lane, 0.0, pltpu.roll(v, cols - 1, 1))
        left = lambda v: jnp.where(first_lane, 0.0, pltpu.roll(v, 1, 1))
        deeper = jnp.where(last_level, 0.0, pltpu.roll(current, depth - 1, 0))
        higher = jnp.where(first_level, 0.0, pltpu.roll(current, 1, 0))
        slope = deeper - higher
        flat = right(current) + left(current)
        if above is not None:
            flat = flat + above
        if below is not None:
            flat = flat + below
        mixed = right(slope) - left(slope)
        new = coef[0, i] * current + coef[1, i] * flat + coef[2, i] * (deeper + higher)
        new = new + coef[3, i] * mixed
        return new if old is None else new - old

    def inject(step, f, i, new):
        if f == 0:
            added = jnp.where(surface_lane == src_cell[0] - lines[i] * cols, wavelet[step], 0.0)
        else:
            at = i * PARTS * STEPS + step
            added = surf[at : at + 1, :]
            for p in range(1, 3):
                added = added + surf[at + p * STEPS : at + p * STEPS + 1, :]
        return new + jnp.where(first_level, added, 0.0)

    for load in loads[2:]:
        load.wait()
    fac_send[0] = facies[odd].astype(jnp.float32).astype(jnp.bfloat16)
    fac_send[1] = facies[even].astype(jnp.float32).astype(jnp.bfloat16)
    fill_coef(0, facies[odd])
    for f in range(2):
        new = advance(0, own[f, odd], None, own[f, even], prev[f, odd])
        trace_send[0, f] = inject(0, f, 0, new)
    fill_coef(1, facies[even])

    reach = min(REACH, tiles - 1)
    pl.semaphore_wait(barrier, jnp.minimum(me, reach) + jnp.minimum(tiles - 1 - me, reach))

    for copy in mate_first:
        copy.start()

    @pl.when(has_far)
    def _():
        for copy in far_first:
            copy.start()

    if reaches:
        signal_at(near_sem.at[0], reaches[0])

    blocks[group : 2 * group, :] = jnp.zeros((group, cols), jnp.float32)
    blocks[group * tiles : group * (tiles + 1), :] = jnp.zeros((group, cols), jnp.float32)
    zero_lines = jnp.zeros((per, LINES, cols), jnp.float32)
    for k in range(NLAG):
        last_own[k] = zero_lines
        last_sum[k] = zero_lines

    for copy in mate_first:
        copy.wait_recv()
    fill_coef(2, mate_fac[...])
    for f in range(2):
        work[0, f] = inject(
            0, f, 1, advance(1, own[f, even], own[f, odd], mate_now[f, odd], prev[f, even])
        )
        work[1, f] = inject(
            0, f, 2, advance(2, mate_now[f, odd], own[f, even], mate_now[f, even], mate_prev[f])
        )
    for f in range(2):
        one = trace_send[0, f]
        new = inject(1, f, 0, advance(0, one, None, work[0, f], own[f, odd]))
        trace_send[1, f] = new
        near = inject(1, f, 1, advance(1, work[0, f], one, work[1, f], own[f, even]))
        work[2, f] = near
        trace_send[2, f] = inject(2, f, 0, advance(0, new, None, near, one))

    @pl.when(has_far)
    def _():
        far_second.start()

    if reaches:
        wait_at(near_sem.at[0], reaches[0])
    if len(reaches) > 1:
        signal_at(near_sem.at[1], reaches[1])

    @pl.when(has_far)
    def _():
        for copy in far_first:
            copy.wait_recv()

    fill_coef(3, fac_recv[0].astype(jnp.float32))
    for f in range(2):
        push = coef[1, 0] * trace_recv[0, f]
        one = trace_send[0, f] + push
        echo = coef[1, 3] * own[f, odd]
        new = advance(0, one, trace_recv[1, f] + echo, work[0, f], own[f, odd])
        two[f, odd] = inject(1, f, 0, new)
        two[f, even] = work[2, f] + coef[1, 1] * push
        work[3, f] = one
        work[4, f] = echo
    mate_second.start()

    def pack_snapshot(s, source):
        for r in range(rows):
            for f in range(2):
                at = (r * 2 + f) * (per + 2)
                upper = source[f, r, pl.ds(0, tiles, stride=2), :]
                lower = source[f, r, pl.ds(1, tiles, stride=2), :]
                blocks[pl.ds(at + 2 * group, tiles, stride=group), :] = lower
                blocks[pl.ds(at + group + 1, tiles, stride=group), :] = upper
                blocks[pl.ds(at + group + 2, tiles, stride=group), :] = lower
                blocks[pl.ds(at + 3, tiles, stride=group), :] = upper
        for d in range(tiles):
            at = (d + 1) * group
            send[s, d] = blocks[at : at + group, :].astype(jnp.bfloat16)

    def snap_copy(s, peer):
        return remote(
            send.at[s, peer], recv.at[s, me], snap_send.at[s, peer], snap_recv.at[s, me], peer
        )

    def each_peer(action):
        def body(peer):
            @pl.when(peer != me)
            def _():
                action(peer)

        in_order(tiles, body)

    def send_snapshot(s):
        each_peer(lambda peer: snap_copy(s, peer).start())
        recv[s, me] = send[s, me]

    pack_snapshot(0, two)
    for n in range(1, len(reaches)):
        wait_at(near_sem.at[n], reaches[n])
        if n + 1 < len(reaches):
            signal_at(near_sem.at[n + 1], reaches[n + 1])
    send_snapshot(0)

    far_two[...] = looked_up(fac_recv[1].astype(jnp.float32))[1]
    for f in range(2):
        work[5, f] = advance(3, work[4, f], work[3, f], None, None)

    @pl.when(has_far)
    def _():
        far_second.wait_recv()

    for f in range(2):
        echo, echo_two = work[4, f], work[5, f]
        new = advance(0, two[f, odd], trace_recv[2, f] + echo_two, two[f, even], work[3, f])
        work[6, f] = inject(2, f, 0, new)
        behind = far_two[...] * echo
        work[7, f] = trace_recv[3, f] + advance(3, echo_two, two[f, odd], behind, echo)

    mate_second.wait_recv()
    for f in range(2):
        near = inject(
            2, f, 1, advance(1, two[f, even], two[f, odd], mate_two[f, odd], work[0, f])
        )
        beyond = inject(
            2, f, 2, advance(2, mate_two[f, odd], two[f, even], mate_two[f, even], work[1, f])
        )
        edge = work[6, f]
        wave_out[f, odd] = inject(3, f, 0, advance(0, edge, work[7, f], near, two[f, odd]))
        wave_out[f, even] = inject(3, f, 1, advance(1, near, edge, beyond, two[f, even]))
    pack_snapshot(1, wave_out)
    send_snapshot(1)

    image_lane = lax.broadcasted_iota(jnp.int32, (1, cols), 1)
    line = lax.broadcasted_iota(jnp.int32, (LINES, cols), 0)
    last_line = line == LINES - 1

    def arrived(s, g):
        for i in range(members):
            peer = g * members + i

            @pl.when(peer != me)
            def _():
                remote(
                    send.at[s, me], recv.at[s, peer], snap_send.at[s, me], snap_recv.at[s, peer], peer
                ).wait_recv()

        for i in range(members):
            staged[s, i * group : (i + 1) * group, :] = recv[s, g * members + i].astype(jnp.float32)
        lifted = lambda f, j: staged[
            s, pl.ds(f * (per + 2) + j, LINES, stride=2 * (per + 2)), :
        ]
        return [
            [
                jnp.concatenate([lifted(f, j), lifted(f, j + 1)], axis=0)
                for j in range(0, per + 2, 2)
            ]
            for f in range(2)
        ]

    def turned(values, amount):
        amount = amount % cols
        return pltpu.roll(values, amount, 1) if amount else values

    def first_products(g):
        ahead, behind = arrived(0, g)
        behind = [v.astype(jnp.bfloat16) for v in behind]
        for k in range(NLAG):
            for j in range(pairs):
                pulled = turned(behind[j], 2 * (margin - k)).astype(jnp.float32)
                part_image[g, k, j] = ahead[j] * pulled

    def finish(g, last):
        ahead, behind = arrived(1, g)
        behind = [v.astype(jnp.bfloat16) for v in behind]

        def write(slot, h, at, results):
            for z in range(per):
                woven[slot, pl.ds(z, LINES, stride=per), :] = results[z]
            out[h + margin, at] = turned(woven[slot].astype(jnp.bfloat16), h)

        for k in range(NLAG):
            h = k - margin
            products = [
                part_image[g, k, j] + ahead[j] * turned(behind[j], -2 * h).astype(jnp.float32)
                for j in range(pairs)
            ]
            if h > 0:
                products = [jnp.where(image_lane < cols - 2 * h, v, 0.0) for v in products]
            elif h < 0:
                products = [jnp.where(image_lane >= -2 * h, v, 0.0) for v in products]
            image = jnp.concatenate(products, axis=0)
            image = image.astype(jnp.bfloat16).astype(jnp.float32)
            plane = [image[j * LINES : (j + 1) * LINES] for j in range(per + 2)]
            before, sums = [], []
            for z in range(per):
                mine = plane[z + 1]
                lower, higher = turned(mine, 1), turned(mine, -1)
                if h == 0:
                    lower = jnp.where(image_lane == 0, 0.0, lower)
                    higher = jnp.where(image_lane == cols - 1, 0.0, higher)
                total = (lower + higher) + (plane[z] + plane[z + 2])
                total = total + pltpu.roll(jnp.where(last_line, last_own[k, z], mine), 1, 0)
                later = pltpu.roll(mine, LINES - 1, 0)
                total = total + jnp.where(last_line, 0.0, later)
                before.append(0.125 * (last_sum[k, z] - jnp.where(last_line, later, 0.0)))
                sums.append(6.0 * mine - total)
            if last:
                if ngroups > 1:
                    write(2 * k, h, g - 1, before)
                write(2 * k + 1, h, g, [0.125 * value for value in sums])
            else:
                write(2 * k, h, jnp.maximum(g - 1, 0), before)
                for z in range(per):
                    last_own[k, z] = plane[z + 1]
                    last_sum[k, z] = sums[z]

    first_products(0)

    def both(g):
        first_products(g + 1)
        finish(g, False)

    in_order(ngroups - 1, both)
    finish(ngroups - 1, True)

    for copy in mate_first:
        copy.wait_send()
    mate_second.wait_send()

    @pl.when(has_far)
    def _():
        for copy in far_first:
            copy.wait_send()
        far_second.wait_send()

    for s in range(2):
        each_peer(lambda peer: snap_copy(s, peer).wait_send())


def shards(tiles, now, prev, facies, vel, eps, tilt, src_cell, wavelet, cells, data):
    rows, depth, cols = facies.shape
    per = depth // tiles
    nrec = cells.shape[0]
    group = 2 * rows * (per + 2)
    ngroups = tiles * rows // LINES
    assert rows == 2 and per == 2 and tiles * rows % LINES == 0
    f32 = jnp.float32
    vmem = pl.BlockSpec(memory_space=pltpu.VMEM)
    hbm = pl.BlockSpec(memory_space=pltpu.HBM)
    lhs_rows = 3 * PARTS * STEPS
    plane = (depth, cols)
    filtered, wave = pl.pallas_call(
        functools.partial(kernel, tiles),
        out_shape=(
            pltpu.VMEM((NLAG, ngroups, LINES * per, cols), jnp.bfloat16),
            pltpu.VMEM(now.shape, f32),
        ),
        in_specs=[hbm] * 10,
        out_specs=(vmem, vmem),
        scratch_shapes=[
            pltpu.VMEM(now.shape, f32),
            pltpu.VMEM(prev.shape, f32),
            pltpu.VMEM(facies.shape, jnp.int32),
            pltpu.SMEM(vel.shape, f32),
            pltpu.SMEM(eps.shape, f32),
            pltpu.SMEM(tilt.shape, f32),
            pltpu.SMEM(src_cell.shape, jnp.int32),
            pltpu.SMEM(wavelet.shape, f32),
            pltpu.VMEM((1, nrec), jnp.int32),
            pltpu.VMEM(data.shape, f32),
            pltpu.VMEM(now.shape, f32),
            pltpu.VMEM((2, *plane), f32),
            pltpu.VMEM(plane, jnp.int32),
            pltpu.VMEM(now.shape, f32),
            pltpu.VMEM((3, 2, *plane), f32),
            pltpu.VMEM((4, 2, *plane), f32),
            pltpu.VMEM((2, *plane), jnp.bfloat16),
            pltpu.VMEM((2, *plane), jnp.bfloat16),
            pltpu.VMEM(now.shape, f32),
            pltpu.VMEM((8, 2, *plane), f32),
            pltpu.VMEM((4, 4, *plane), f32),
            pltpu.VMEM(plane, f32),
            pltpu.VMEM((lhs_rows, nrec), f32),
            pltpu.VMEM((lhs_rows, cols), f32),
            pltpu.VMEM(((tiles + 2) * group, cols), f32),
            pltpu.VMEM((2, tiles, group, cols), jnp.bfloat16),
            pltpu.VMEM((2, tiles, group, cols), jnp.bfloat16),
            pltpu.VMEM((2, LINES // rows * group, cols), f32),
            pltpu.VMEM((ngroups, NLAG, (per + 2) // 2, 2 * LINES, cols), f32),
            pltpu.VMEM((NLAG, per, LINES, cols), f32),
            pltpu.VMEM((NLAG, per, LINES, cols), f32),
            pltpu.VMEM((2 * NLAG, LINES * per, cols), f32),
            pltpu.SemaphoreType.DMA((4,)),
            pltpu.SemaphoreType.DMA((4,)),
            pltpu.SemaphoreType.DMA((4,)),
            pltpu.SemaphoreType.DMA((4,)),
            pltpu.SemaphoreType.DMA((2, tiles)),
            pltpu.SemaphoreType.DMA((2, tiles)),
            pltpu.SemaphoreType.DMA((10,)),
            pltpu.SemaphoreType.REGULAR((max(1, tiles.bit_length()),)),
        ],
        compiler_params=pltpu.CompilerParams(collective_id=0, has_side_effects=True),
    )(now, prev, facies, vel, eps, tilt, src_cell, wavelet, cells.reshape(1, nrec), data)
    return filtered.reshape(NLAG, rows * tiles, per, cols), wave


def solution(mesh):
    return jax.shard_map(
        functools.partial(shards, mesh.shape["tile"]),
        mesh=mesh,
        in_specs=(
            P("shot", "tile", None, None),
            P("shot", "tile", None, None),
            P("tile", None, None),
            P(),
            P(),
            P(),
            P("shot"),
            P("shot"),
            P("shot"),
            P(None, "shot"),
        ),
        out_specs=(P("shot", None, "tile", None), P("shot", "tile", None, None)),
        check_vma=False,
    )
```

time: 23.4 us -> 19.2 us (0.82)
  Pallas kernels: 20.5 us -> 16.3 us
    pallas_call x1, Pallas kernels: 20.5 us -> 16.3 us  [shards(): pl.pallas_call(functools.partial(kernel, tiles), out_shape=(pltpu.VMEM((N...]
where the time goes in v1:
time: 19.2 us; the launch traced here: 19 us
  Pallas kernels  16.3 us (85%)
  local copies, waits for them, and re-layouts  1.42 us (7%)
  between operations  1.29 us (7%)
    pallas_call x1, Pallas kernels, shards(): pl.pallas_call(functools.partial(kernel, tiles), out_shape=(pltpu.VMEM((N...  16.3 us
    unnamed x2, local copies, waits for them, and re-layouts  1.42 us

profile of v1, /device:TPU:0, one launch (start us, length us, event | category | flops | bytes accessed | tf_op | source)
XLA Modules:
  0.0 19.0 jit_solution(5504333430891958716)
XLA Ops:
  1.3 16.3 %shard_map.113 = (bf16[32,4,16,128]{3,2,1,0:T(8,128)(2,1)S(1)}, f32[2,2,32,128]{3,2,1,0:T(8,128)S(1)}) custom-call(f32[2,2,32,128]{3,2,1,0:T(8,128)} %now.1, f32[2,2,32,128]{3,2,1,0:T(8,128)} %prev_in.1, s32[2,32,128]{2,1,0:T(8,128)} %facies_in.1, f32[8]{0:T(128)} %vel_in.1, f32[8]{0:T(128)} %eps_in.1, f32[8]{0:T(128)} %tilt_in.1, s32[1]{0:T(128)S(6)} %copy.16.src_in, ...), custom_call_target="tpu_custom_call" | custom-call | tf_op jit(solution)/shard_map/pallas_call | solution.py:505
  17.6 0.8 %copy.14 = bf16[32,32,2,128]{3,2,1,0:T(2,128)(2,1)} copy(bf16[32,32,2,128]{3,2,1,0:T(2,128)(2,1)S(1)} %bitcast.2) | data formatting | bytes 1048576
  18.4 0.6 %copy.15 = f32[2,2,32,128]{3,2,1,0:T(8,128)} copy(f32[2,2,32,128]{3,2,1,0:T(8,128)S(1)} %get-tuple-element.7) | data formatting | bytes 131072

commit v2 on v1

--- a/solution.py
+++ b/solution.py
@@ -92,47 +92,47 @@
     far = me - 1 + 2 * odd
     has_far = (far >= 0) & (far < tiles)
 
-    barrier = pltpu.get_barrier_semaphore()
-
-    def signal_at(semaphore, step):
-        for way in (-step, step):
-            peer = me + way
-            there = (peer >= 0) & (peer < tiles)
-
-            @pl.when(there)
-            def _():
-                pl.semaphore_signal(semaphore, inc=1, device_id={"tile": peer})
-
-    def wait_at(semaphore, step):
-        lower = (me >= step).astype(jnp.int32)
-        pl.semaphore_wait(semaphore, lower + (me + step < tiles).astype(jnp.int32))
-
-    for step in range(1, min(REACH, tiles - 1) + 1):
-        signal_at(barrier, step)
-
-    reaches = []
-    while (REACH << len(reaches)) < tiles - 1:
-        reaches.append(REACH << len(reaches))
-
     loads = [
         pltpu.make_async_copy(src, dst, load_sem.at[n])
         for n, (src, dst) in enumerate(
             (
-                (cells_in, cells),
-                (data_in, data),
+                (now, own),
+                (prev_in, prev),
                 (facies_in, facies),
                 (vel_in, vel_tab),
                 (eps_in, eps_tab),
                 (tilt_in, tilt_tab),
+                (cells_in, cells),
+                (data_in, data),
                 (src_in, src_cell),
                 (wavelet_in, wavelet),
-                (now, own),
-                (prev_in, prev),
             )
         )
     ]
     for load in loads:
         load.start()
+    barrier = pltpu.get_barrier_semaphore()
+
+    def signal_at(semaphore, step):
+        for way in (-step, step):
+            peer = me + way
+            there = (peer >= 0) & (peer < tiles)
+
+            @pl.when(there)
+            def _():
+                pl.semaphore_signal(semaphore, inc=1, device_id={"tile": peer})
+
+    def wait_at(semaphore, step):
+        lower = (me >= step).astype(jnp.int32)
+        pl.semaphore_wait(semaphore, lower + (me + step < tiles).astype(jnp.int32))
+
+    for step in range(1, min(REACH, tiles - 1) + 1):
+        signal_at(barrier, step)
+
+    reaches = []
+    while (REACH << len(reaches)) < tiles - 1:
+        reaches.append(REACH << len(reaches))
+
     zero_plane = jnp.zeros((depth, cols), jnp.float32)
 
     @pl.when(jnp.logical_not(has_far))
@@ -160,16 +160,99 @@
         mate_copy(2, facies.at[even], mate_fac),
     )
     mate_second = mate_copy(3, two, mate_two)
-    far_first = (
-        far_copy(0, fac_send, fac_recv),
-        far_copy(1, own.at[:, odd], trace_recv.at[0]),
-        far_copy(2, trace_send.at[0], trace_recv.at[1]),
+    far_fac = far_copy(0, fac_send.at[0], fac_recv.at[0])
+    far_deep = far_copy(1, fac_send.at[1], fac_recv.at[1])
+    far_now = far_copy(2, own.at[:, odd], trace_recv.at[0])
+    far_one, far_second, far_third = (
+        far_copy(3 + k, trace_send.at[k], trace_recv.at[k + 1]) for k in range(3)
     )
-    far_second = far_copy(3, trace_send.at[1:3], trace_recv.at[2:4])
-
-    lines = (me * rows + odd, me * rows + even, mate * rows + odd)
-
-    for load in loads[:2]:
+    far_all = (far_fac, far_now, far_one, far_deep, far_second, far_third)
+
+    def from_far(*copies):
+        @pl.when(has_far)
+        def _():
+            for copy in copies:
+                copy.wait_recv()
+
+    def to_far(*copies):
+        @pl.when(has_far)
+        def _():
+            for copy in copies:
+                copy.start()
+
+    lines = (me * rows + odd, me * rows + even, mate * rows + odd, far * rows + even)
+
+    def looked_up(kinds):
+        vel = jnp.zeros((depth, cols), jnp.float32)
+        eps, tlt = vel, vel
+        for n in range(vel_tab.shape[0]):
+            here = kinds == n
+            vel = jnp.where(here, vel_tab[n], vel)
+            eps = jnp.where(here, eps_tab[n], eps)
+            tlt = jnp.where(here, tilt_tab[n], tlt)
+        return vel, vel * (1.0 + 2.0 * eps), 0.25 * vel * tlt
+
+    lane = lax.broadcasted_iota(jnp.int32, (depth, cols), 1)
+    level = lax.broadcasted_iota(jnp.int32, (depth, cols), 0)
+    first_lane, last_lane = lane == 0, lane == cols - 1
+    first_level, last_level = level == 0, level == depth - 1
+    surface_lane = lax.broadcasted_iota(jnp.int32, (1, cols), 1)
+
+    to_right = lambda v: pltpu.roll(v, 1, 1)
+    to_left = lambda v: pltpu.roll(v, cols - 1, 1)
+
+    def fill_coef(i, kinds):
+        vel, flat, tlt = looked_up(kinds)
+        coef[0, i] = 2.0 - 4.0 * flat - 2.0 * vel
+        coef[1, i] = flat
+        coef[2, i] = vel
+        coef[3, i] = jnp.where(first_lane, 0.0, to_right(flat))
+        coef[4, i] = jnp.where(first_lane, 0.0, to_right(tlt))
+        coef[5, i] = jnp.where(last_lane, 0.0, to_left(flat))
+        coef[6, i] = jnp.where(last_lane, 0.0, to_left(tlt))
+
+    def advance(i, current, above, below, old):
+        deeper = jnp.where(last_level, 0.0, pltpu.roll(current, depth - 1, 0))
+        higher = jnp.where(first_level, 0.0, pltpu.roll(current, 1, 0))
+        slope = deeper - higher
+        new = to_left(coef[3, i] * current + coef[4, i] * slope)
+        new = new + to_right(coef[5, i] * current - coef[6, i] * slope)
+        new = new + coef[2, i] * (deeper + higher) + coef[0, i] * current
+        if above is not None:
+            new = new + coef[1, i] * (above if below is None else above + below)
+        elif below is not None:
+            new = new + coef[1, i] * below
+        return new if old is None else new - old
+
+    def inject(step, f, i, new):
+        if f == 0:
+            added = jnp.where(surface_lane == src_cell[0] - lines[i] * cols, wavelet[step], 0.0)
+        else:
+            at = i * PARTS * STEPS + step
+            added = surf[at : at + 1, :]
+            for p in range(1, 3):
+                added = added + surf[at + p * STEPS : at + p * STEPS + 1, :]
+        return new + jnp.where(first_level, added, 0.0)
+
+    for load in loads[:6]:
+        load.wait()
+    fac_send[0] = facies[odd].astype(jnp.float32).astype(jnp.bfloat16)
+    fac_send[1] = facies[even].astype(jnp.float32).astype(jnp.bfloat16)
+    fill_coef(0, facies[odd])
+    for f in range(2):
+        trace_send[0, f] = advance(0, own[f, odd], None, own[f, even], prev[f, odd])
+    reach = min(REACH, tiles - 1)
+    pl.semaphore_wait(barrier, jnp.minimum(me, reach) + jnp.minimum(tiles - 1 - me, reach))
+
+    to_far(far_fac, far_now, far_one)
+    for copy in mate_first:
+        copy.start()
+    to_far(far_deep)
+
+    if reaches:
+        signal_at(near_sem.at[0], reaches[0])
+
+    for load in loads[6:]:
         load.wait()
 
     cell = cells[...]
@@ -181,7 +264,7 @@
     rest = amounts - high
     middle = rest.astype(jnp.bfloat16).astype(jnp.float32)
     parts = (high, middle, rest - middle, jnp.zeros_like(high))
-    for i in range(3):
+    for i in range(4):
         first = lines[i] * cols
         inside = (cell >= first) & (cell < first + cols)
         for p, part in enumerate(parts):
@@ -192,79 +275,9 @@
         preferred_element_type=jnp.float32,
     )
 
-    def looked_up(kinds):
-        vel = jnp.zeros((depth, cols), jnp.float32)
-        eps, tlt = vel, vel
-        for n in range(vel_tab.shape[0]):
-            here = kinds == n
-            vel = jnp.where(here, vel_tab[n], vel)
-            eps = jnp.where(here, eps_tab[n], eps)
-            tlt = jnp.where(here, tilt_tab[n], tlt)
-        return vel, vel * (1.0 + 2.0 * eps), 0.25 * vel * tlt
-
-    def fill_coef(i, kinds):
-        vel, flat, tlt = looked_up(kinds)
-        coef[0, i] = 2.0 - 4.0 * flat - 2.0 * vel
-        coef[1, i] = flat
-        coef[2, i] = vel
-        coef[3, i] = tlt
-
-    lane = lax.broadcasted_iota(jnp.int32, (depth, cols), 1)
-    level = lax.broadcasted_iota(jnp.int32, (depth, cols), 0)
-    first_lane, last_lane = lane == 0, lane == cols - 1
-    first_level, last_level = level == 0, level == depth - 1
-    surface_lane = lax.broadcasted_iota(jnp.int32, (1, cols), 1)
-
-    def advance(i, current, above, below, old):
-        right = lambda v: jnp.where(last_lane, 0.0, pltpu.roll(v, cols - 1, 1))
-        left = lambda v: jnp.where(first_lane, 0.0, pltpu.roll(v, 1, 1))
-        deeper = jnp.where(last_level, 0.0, pltpu.roll(current, depth - 1, 0))
-        higher = jnp.where(first_level, 0.0, pltpu.roll(current, 1, 0))
-        slope = deeper - higher
-        flat = right(current) + left(current)
-        if above is not None:
-            flat = flat + above
-        if below is not None:
-            flat = flat + below
-        mixed = right(slope) - left(slope)
-        new = coef[0, i] * current + coef[1, i] * flat + coef[2, i] * (deeper + higher)
-        new = new + coef[3, i] * mixed
-        return new if old is None else new - old
-
-    def inject(step, f, i, new):
-        if f == 0:
-            added = jnp.where(surface_lane == src_cell[0] - lines[i] * cols, wavelet[step], 0.0)
-        else:
-            at = i * PARTS * STEPS + step
-            added = surf[at : at + 1, :]
-            for p in range(1, 3):
-                added = added + surf[at + p * STEPS : at + p * STEPS + 1, :]
-        return new + jnp.where(first_level, added, 0.0)
-
-    for load in loads[2:]:
-        load.wait()
-    fac_send[0] = facies[odd].astype(jnp.float32).astype(jnp.bfloat16)
-    fac_send[1] = facies[even].astype(jnp.float32).astype(jnp.bfloat16)
-    fill_coef(0, facies[odd])
-    for f in range(2):
-        new = advance(0, own[f, odd], None, own[f, even], prev[f, odd])
-        trace_send[0, f] = inject(0, f, 0, new)
+    for f in range(2):
+        work[3, f] = inject(0, f, 0, trace_send[0, f])
     fill_coef(1, facies[even])
-
-    reach = min(REACH, tiles - 1)
-    pl.semaphore_wait(barrier, jnp.minimum(me, reach) + jnp.minimum(tiles - 1 - me, reach))
-
-    for copy in mate_first:
-        copy.start()
-
-    @pl.when(has_far)
-    def _():
-        for copy in far_first:
-            copy.start()
-
-    if reaches:
-        signal_at(near_sem.at[0], reaches[0])
-
     blocks[group : 2 * group, :] = jnp.zeros((group, cols), jnp.float32)
     blocks[group * tiles : group * (tiles + 1), :] = jnp.zeros((group, cols), jnp.float32)
     zero_lines = jnp.zeros((per, LINES, cols), jnp.float32)
@@ -272,44 +285,41 @@
         last_own[k] = zero_lines
         last_sum[k] = zero_lines
 
-    for copy in mate_first:
-        copy.wait_recv()
-    fill_coef(2, mate_fac[...])
+    mate_first[0].wait_recv()
     for f in range(2):
         work[0, f] = inject(
             0, f, 1, advance(1, own[f, even], own[f, odd], mate_now[f, odd], prev[f, even])
         )
+        trace_send[1, f] = inject(
+            1, f, 0, advance(0, work[3, f], None, work[0, f], own[f, odd])
+        )
+    to_far(far_second)
+    for copy in mate_first[1:]:
+        copy.wait_recv()
+    fill_coef(2, mate_fac[...])
+    for f in range(2):
         work[1, f] = inject(
             0, f, 2, advance(2, mate_now[f, odd], own[f, even], mate_now[f, even], mate_prev[f])
         )
-    for f in range(2):
-        one = trace_send[0, f]
-        new = inject(1, f, 0, advance(0, one, None, work[0, f], own[f, odd]))
-        trace_send[1, f] = new
-        near = inject(1, f, 1, advance(1, work[0, f], one, work[1, f], own[f, even]))
+        near = inject(1, f, 1, advance(1, work[0, f], work[3, f], work[1, f], own[f, even]))
         work[2, f] = near
-        trace_send[2, f] = inject(2, f, 0, advance(0, new, None, near, one))
-
-    @pl.when(has_far)
-    def _():
-        far_second.start()
+        trace_send[2, f] = inject(2, f, 0, advance(0, trace_send[1, f], None, near, work[3, f]))
+    to_far(far_third)
 
     if reaches:
         wait_at(near_sem.at[0], reaches[0])
     if len(reaches) > 1:
         signal_at(near_sem.at[1], reaches[1])
 
-    @pl.when(has_far)
-    def _():
-        for copy in far_first:
-            copy.wait_recv()
+    from_far(far_fac, far_now, far_one)
 
     fill_coef(3, fac_recv[0].astype(jnp.float32))
     for f in range(2):
         push = coef[1, 0] * trace_recv[0, f]
-        one = trace_send[0, f] + push
+        one = work[3, f] + push
         echo = coef[1, 3] * own[f, odd]
-        new = advance(0, one, trace_recv[1, f] + echo, work[0, f], own[f, odd])
+        beside = inject(0, f, 3, trace_recv[1, f]) + echo
+        new = advance(0, one, beside, work[0, f], own[f, odd])
         two[f, odd] = inject(1, f, 0, new)
         two[f, even] = work[2, f] + coef[1, 1] * push
         work[3, f] = one
@@ -354,32 +364,32 @@
             signal_at(near_sem.at[n + 1], reaches[n + 1])
     send_snapshot(0)
 
+    from_far(far_deep)
     far_two[...] = looked_up(fac_recv[1].astype(jnp.float32))[1]
     for f in range(2):
-        work[5, f] = advance(3, work[4, f], work[3, f], None, None)
-
-    @pl.when(has_far)
-    def _():
-        far_second.wait_recv()
-
-    for f in range(2):
-        echo, echo_two = work[4, f], work[5, f]
-        new = advance(0, two[f, odd], trace_recv[2, f] + echo_two, two[f, even], work[3, f])
+        echo = work[4, f]
+        echo_two = advance(3, echo, work[3, f], None, None)
+        work[5, f] = advance(3, echo_two, two[f, odd], far_two[...] * echo, echo)
+        new = advance(0, two[f, odd], echo_two, two[f, even], work[3, f])
         work[6, f] = inject(2, f, 0, new)
-        behind = far_two[...] * echo
-        work[7, f] = trace_recv[3, f] + advance(3, echo_two, two[f, odd], behind, echo)
-
+        new = advance(1, two[f, even], two[f, odd], None, work[0, f])
+        work[7, f] = inject(2, f, 1, new)
+
+    from_far(far_second)
+    for f in range(2):
+        work[6, f] = work[6, f] + coef[1, 0] * trace_recv[2, f]
     mate_second.wait_recv()
     for f in range(2):
-        near = inject(
-            2, f, 1, advance(1, two[f, even], two[f, odd], mate_two[f, odd], work[0, f])
-        )
+        edge = work[6, f]
+        near = work[7, f] + coef[1, 1] * mate_two[f, odd]
         beyond = inject(
             2, f, 2, advance(2, mate_two[f, odd], two[f, even], mate_two[f, even], work[1, f])
         )
-        edge = work[6, f]
-        wave_out[f, odd] = inject(3, f, 0, advance(0, edge, work[7, f], near, two[f, odd]))
+        wave_out[f, odd] = inject(3, f, 0, advance(0, edge, work[5, f], near, two[f, odd]))
         wave_out[f, even] = inject(3, f, 1, advance(1, near, edge, beyond, two[f, even]))
+    from_far(far_third)
+    for f in range(2):
+        wave_out[f, odd] = wave_out[f, odd] + coef[1, 0] * trace_recv[3, f]
     pack_snapshot(1, wave_out)
     send_snapshot(1)
 
@@ -474,20 +484,29 @@
         finish(g, False)
 
     in_order(ngroups - 1, both)
-    finish(ngroups - 1, True)
-
     for copy in mate_first:
         copy.wait_send()
     mate_second.wait_send()
 
     @pl.when(has_far)
     def _():
-        for copy in far_first:
+        for copy in far_all:
             copy.wait_send()
-        far_second.wait_send()
 
     for s in range(2):
         each_peer(lambda peer: snap_copy(s, peer).wait_send())
+
+    finish(ngroups - 1, True)
+
+def stored(filtered_in, wave_in, filtered, wave, sems):
+    copies = [
+        pltpu.make_async_copy(src, dst, sems.at[n])
+        for n, (src, dst) in enumerate(((filtered_in, filtered), (wave_in, wave)))
+    ]
+    for copy in copies:
+        copy.start()
+    for copy in copies:
+        copy.wait()
 
 
 def shards(tiles, now, prev, facies, vel, eps, tilt, src_cell, wavelet, cells, data):
@@ -500,7 +519,7 @@
     f32 = jnp.float32
     vmem = pl.BlockSpec(memory_space=pltpu.VMEM)
     hbm = pl.BlockSpec(memory_space=pltpu.HBM)
-    lhs_rows = 3 * PARTS * STEPS
+    lhs_rows = 4 * PARTS * STEPS
     plane = (depth, cols)
     filtered, wave = pl.pallas_call(
         functools.partial(kernel, tiles),
@@ -531,7 +550,7 @@
             pltpu.VMEM((2, *plane), jnp.bfloat16),
             pltpu.VMEM(now.shape, f32),
             pltpu.VMEM((8, 2, *plane), f32),
-            pltpu.VMEM((4, 4, *plane), f32),
+            pltpu.VMEM((7, 4, *plane), f32),
             pltpu.VMEM(plane, f32),
             pltpu.VMEM((lhs_rows, nrec), f32),
             pltpu.VMEM((lhs_rows, cols), f32),
@@ -545,8 +564,8 @@
             pltpu.VMEM((2 * NLAG, LINES * per, cols), f32),
             pltpu.SemaphoreType.DMA((4,)),
             pltpu.SemaphoreType.DMA((4,)),
-            pltpu.SemaphoreType.DMA((4,)),
-            pltpu.SemaphoreType.DMA((4,)),
+            pltpu.SemaphoreType.DMA((6,)),
+            pltpu.SemaphoreType.DMA((6,)),
             pltpu.SemaphoreType.DMA((2, tiles)),
             pltpu.SemaphoreType.DMA((2, tiles)),
             pltpu.SemaphoreType.DMA((10,)),
@@ -554,6 +573,17 @@
         ],
         compiler_params=pltpu.CompilerParams(collective_id=0, has_side_effects=True),
     )(now, prev, facies, vel, eps, tilt, src_cell, wavelet, cells.reshape(1, nrec), data)
+    filtered, wave = pl.pallas_call(
+        stored,
+        out_shape=(
+            jax.ShapeDtypeStruct(filtered.shape, jnp.bfloat16),
+            jax.ShapeDtypeStruct(now.shape, f32),
+        ),
+        in_specs=[vmem] * 2,
+        out_specs=(hbm, hbm),
+        scratch_shapes=[pltpu.SemaphoreType.DMA((2,))],
+        compiler_params=pltpu.CompilerParams(vmem_limit_bytes=1 << 20),
+    )(filtered, wave)
     return filtered.reshape(NLAG, rows * tiles, per, cols), wave
 
 

time: 19.2 us -> 18.2 us (0.948)
  local copies, waits for them, and re-layouts: 1.42 us -> 0 us
  Pallas kernels: 16.3 us -> 16.7 us
    unnamed x2 -> x0, local copies, waits for them, and re-layouts: 1.42 us -> none
    pallas_call x0 -> x1, Pallas kernels: none -> 0.82 us  [shards(): pl.pallas_call(stored, out_shape=(jax.ShapeDtypeStruct(filtered.shape, jn...]
    pallas_call x1, Pallas kernels: 16.3 us -> 15.9 us  [shards(): pl.pallas_call(functools.partial(kernel, tiles), out_shape=(pltpu.VMEM((N...]
where the time goes in v2:
time: 18.2 us; the launch traced here: 18 us
  Pallas kernels  16.7 us (92%)
  between operations  1.29 us (7%)
    pallas_call x1, Pallas kernels, shards(): pl.pallas_call(functools.partial(kernel, tiles), out_shape=(pltpu.VMEM((N...  15.9 us
    pallas_call x1, Pallas kernels, shards(): pl.pallas_call(stored, out_shape=(jax.ShapeDtypeStruct(filtered.shape, jn...  0.82 us

profile of v2, /device:TPU:0, one launch (start us, length us, event | category | flops | bytes accessed | tf_op | source)
XLA Modules:
  0.0 18.0 jit_solution(8089327278529545570)
XLA Ops:
  1.3 15.9 %shard_map.113 = (bf16[32,4,16,128]{3,2,1,0:T(8,128)(2,1)S(1)}, f32[2,2,32,128]{3,2,1,0:T(8,128)S(1)}) custom-call(f32[2,2,32,128]{3,2,1,0:T(8,128)} %now.1, f32[2,2,32,128]{3,2,1,0:T(8,128)} %prev_in.1, s32[2,32,128]{2,1,0:T(8,128)} %facies_in.1, f32[8]{0:T(128)} %vel_in.1, f32[8]{0:T(128)} %eps_in.1, f32[8]{0:T(128)} %tilt_in.1, s32[1]{0:T(128)S(6)} %copy.12.src_in, ...), custom_call_target="tpu_custom_call" | custom-call | tf_op jit(solution)/shard_map/pallas_call | solution.py:524
  17.2 0.8 %shard_map.114 = (bf16[32,4,16,128]{3,2,1,0:T(8,128)(2,1)}, f32[2,2,32,128]{3,2,1,0:T(8,128)}) custom-call(bf16[32,4,16,128]{3,2,1,0:T(8,128)(2,1)S(1)} %get-tuple-element.6.filtered_in, f32[2,2,32,128]{3,2,1,0:T(8,128)S(1)} %get-tuple-element.7.wave_in), custom_call_target="tpu_custom_call" | custom-call | tf_op jit(solution)/shard_map/pallas_call | solution.py:576

commit v3 on v2

--- a/solution.py
+++ b/solution.py
@@ -49,7 +49,8 @@
     mate_now,
     mate_prev,
     mate_fac,
-    mate_two,
+    mate_near,
+    mate_edge,
     trace_send,
     trace_recv,
     fac_send,
@@ -75,7 +76,9 @@
     snap_send,
     snap_recv,
     load_sem,
-    near_sem,
+    entered_sem,
+    below_sem,
+    above_sem,
 ):
     rows, depth, cols = facies.shape
     per = depth // tiles
@@ -92,6 +95,37 @@
     far = me - 1 + 2 * odd
     has_far = (far >= 0) & (far < tiles)
 
+    reaches = []
+    while (REACH << len(reaches)) < tiles - 1:
+        reaches.append(REACH << len(reaches))
+
+    barrier = pltpu.get_barrier_semaphore()
+
+    def signal_at(semaphore, *ways):
+        for way in ways:
+            peer = me + way
+            there = (peer >= 0) & (peer < tiles)
+
+            @pl.when(there)
+            def _():
+                pl.semaphore_signal(semaphore, inc=1, device_id={"tile": peer})
+
+    def tell(n):
+        signal_at(below_sem.at[n], reaches[n])
+        signal_at(above_sem.at[n], -reaches[n])
+
+    def hear_below(n):
+        @pl.when(me >= reaches[n])
+        def _():
+            pl.semaphore_wait(below_sem.at[n], 1)
+
+    def hear_above(n):
+        @pl.when(me + reaches[n] < tiles)
+        def _():
+            pl.semaphore_wait(above_sem.at[n], 1)
+
+    reach = min(REACH, tiles - 1)
+    signal_at(barrier, -1, 1)
     loads = [
         pltpu.make_async_copy(src, dst, load_sem.at[n])
         for n, (src, dst) in enumerate(
@@ -111,27 +145,7 @@
     ]
     for load in loads:
         load.start()
-    barrier = pltpu.get_barrier_semaphore()
-
-    def signal_at(semaphore, step):
-        for way in (-step, step):
-            peer = me + way
-            there = (peer >= 0) & (peer < tiles)
-
-            @pl.when(there)
-            def _():
-                pl.semaphore_signal(semaphore, inc=1, device_id={"tile": peer})
-
-    def wait_at(semaphore, step):
-        lower = (me >= step).astype(jnp.int32)
-        pl.semaphore_wait(semaphore, lower + (me + step < tiles).astype(jnp.int32))
-
-    for step in range(1, min(REACH, tiles - 1) + 1):
-        signal_at(barrier, step)
-
-    reaches = []
-    while (REACH << len(reaches)) < tiles - 1:
-        reaches.append(REACH << len(reaches))
+    signal_at(barrier, *range(2, reach + 1))
 
     zero_plane = jnp.zeros((depth, cols), jnp.float32)
 
@@ -159,7 +173,8 @@
         mate_copy(1, prev.at[:, even], mate_prev),
         mate_copy(2, facies.at[even], mate_fac),
     )
-    mate_second = mate_copy(3, two, mate_two)
+    mate_second = mate_copy(3, two.at[:, even], mate_near)
+    mate_third = mate_copy(4, two.at[:, odd], mate_edge)
     far_fac = far_copy(0, fac_send.at[0], fac_recv.at[0])
     far_deep = far_copy(1, fac_send.at[1], fac_recv.at[1])
     far_now = far_copy(2, own.at[:, odd], trace_recv.at[0])
@@ -234,23 +249,22 @@
                 added = added + surf[at + p * STEPS : at + p * STEPS + 1, :]
         return new + jnp.where(first_level, added, 0.0)
 
-    for load in loads[:6]:
+    loads[0].wait()
+    pl.semaphore_wait(barrier, jnp.minimum(me, reach) + jnp.minimum(tiles - 1 - me, 1))
+    to_far(far_now)
+    mate_first[0].start()
+    for load in loads[1:6]:
         load.wait()
+    for copy in mate_first[1:]:
+        copy.start()
     fac_send[0] = facies[odd].astype(jnp.float32).astype(jnp.bfloat16)
     fac_send[1] = facies[even].astype(jnp.float32).astype(jnp.bfloat16)
     fill_coef(0, facies[odd])
     for f in range(2):
         trace_send[0, f] = advance(0, own[f, odd], None, own[f, even], prev[f, odd])
-    reach = min(REACH, tiles - 1)
-    pl.semaphore_wait(barrier, jnp.minimum(me, reach) + jnp.minimum(tiles - 1 - me, reach))
-
-    to_far(far_fac, far_now, far_one)
-    for copy in mate_first:
-        copy.start()
-    to_far(far_deep)
-
-    if reaches:
-        signal_at(near_sem.at[0], reaches[0])
+    to_far(far_fac, far_one, far_deep)
+
+    signal_at(entered_sem.at[0], *range(-reach, -1))
 
     for load in loads[6:]:
         load.wait()
@@ -306,25 +320,36 @@
         trace_send[2, f] = inject(2, f, 0, advance(0, trace_send[1, f], None, near, work[3, f]))
     to_far(far_third)
 
+    beyond_next = jnp.minimum(tiles - 2 - me, reach - 1)
+
+    @pl.when(beyond_next > 0)
+    def _():
+        pl.semaphore_wait(entered_sem.at[0], beyond_next)
+
     if reaches:
-        wait_at(near_sem.at[0], reaches[0])
+        tell(0)
+
+    from_far(far_fac)
+    fill_coef(3, fac_recv[0].astype(jnp.float32))
     if len(reaches) > 1:
-        signal_at(near_sem.at[1], reaches[1])
-
-    from_far(far_fac, far_now, far_one)
-
-    fill_coef(3, fac_recv[0].astype(jnp.float32))
+        hear_below(0)
+        hear_above(0)
+        tell(1)
+    from_far(far_now)
     for f in range(2):
         push = coef[1, 0] * trace_recv[0, f]
         one = work[3, f] + push
         echo = coef[1, 3] * own[f, odd]
-        beside = inject(0, f, 3, trace_recv[1, f]) + echo
-        new = advance(0, one, beside, work[0, f], own[f, odd])
-        two[f, odd] = inject(1, f, 0, new)
         two[f, even] = work[2, f] + coef[1, 1] * push
+        new = advance(0, one, inject(0, f, 3, echo), work[0, f], own[f, odd])
+        work[8, f] = inject(1, f, 0, new)
         work[3, f] = one
         work[4, f] = echo
     mate_second.start()
+    from_far(far_one)
+    for f in range(2):
+        two[f, odd] = work[8, f] + coef[1, 0] * trace_recv[1, f]
+    mate_third.start()
 
     def pack_snapshot(s, source):
         for r in range(rows):
@@ -339,30 +364,41 @@
         for d in range(tiles):
             at = (d + 1) * group
             send[s, d] = blocks[at : at + group, :].astype(jnp.bfloat16)
-
     def snap_copy(s, peer):
         return remote(
             send.at[s, peer], recv.at[s, me], snap_send.at[s, peer], snap_recv.at[s, me], peer
         )
 
+    def other(peer, action):
+        @pl.when(peer != me)
+        def _():
+            action(peer)
+
     def each_peer(action):
-        def body(peer):
-            @pl.when(peer != me)
-            def _():
-                action(peer)
-
-        in_order(tiles, body)
-
-    def send_snapshot(s):
-        each_peer(lambda peer: snap_copy(s, peer).start())
+        in_order(tiles, lambda peer: other(peer, action))
+
+    def send_to(s, first, end):
+        def run(peer, carry):
+            snap_copy(s, peer).start()
+            return carry
+
+        lax.fori_loop(first, end, run, 0)
+
+    def send_below(s):
+        send_to(s, 0, me)
+
+    def send_above(s):
+        send_to(s, me + 1, tiles)
         recv[s, me] = send[s, me]
 
+    for n in range(1, len(reaches) - 1):
+        hear_below(n)
+        hear_above(n)
+        tell(n + 1)
+    if reaches:
+        hear_below(len(reaches) - 1)
     pack_snapshot(0, two)
-    for n in range(1, len(reaches)):
-        wait_at(near_sem.at[n], reaches[n])
-        if n + 1 < len(reaches):
-            signal_at(near_sem.at[n + 1], reaches[n + 1])
-    send_snapshot(0)
+    send_below(0)
 
     from_far(far_deep)
     far_two[...] = looked_up(fac_recv[1].astype(jnp.float32))[1]
@@ -372,26 +408,34 @@
         work[5, f] = advance(3, echo_two, two[f, odd], far_two[...] * echo, echo)
         new = advance(0, two[f, odd], echo_two, two[f, even], work[3, f])
         work[6, f] = inject(2, f, 0, new)
-        new = advance(1, two[f, even], two[f, odd], None, work[0, f])
+
+    mate_second.wait_recv()
+    for f in range(2):
+        new = advance(1, two[f, even], two[f, odd], mate_near[f], work[0, f])
         work[7, f] = inject(2, f, 1, new)
+        new = advance(2, mate_near[f], two[f, even], None, work[1, f])
+        work[8, f] = inject(2, f, 2, new)
 
     from_far(far_second)
     for f in range(2):
-        work[6, f] = work[6, f] + coef[1, 0] * trace_recv[2, f]
-    mate_second.wait_recv()
-    for f in range(2):
-        edge = work[6, f]
-        near = work[7, f] + coef[1, 1] * mate_two[f, odd]
-        beyond = inject(
-            2, f, 2, advance(2, mate_two[f, odd], two[f, even], mate_two[f, even], work[1, f])
-        )
-        wave_out[f, odd] = inject(3, f, 0, advance(0, edge, work[5, f], near, two[f, odd]))
-        wave_out[f, even] = inject(3, f, 1, advance(1, near, edge, beyond, two[f, even]))
+        edge = work[6, f] + coef[1, 0] * trace_recv[2, f]
+        near = work[7, f]
+        new = advance(0, edge, work[5, f], near, two[f, odd])
+        wave_out[f, odd] = inject(3, f, 0, new)
+        new = advance(1, near, edge, work[8, f], two[f, even])
+        wave_out[f, even] = inject(3, f, 1, new)
+    mate_third.wait_recv()
+    for f in range(2):
+        wave_out[f, even] = wave_out[f, even] + coef[1, 1] * (coef[1, 2] * mate_edge[f])
     from_far(far_third)
     for f in range(2):
         wave_out[f, odd] = wave_out[f, odd] + coef[1, 0] * trace_recv[3, f]
     pack_snapshot(1, wave_out)
-    send_snapshot(1)
+    send_below(1)
+    if reaches:
+        hear_above(len(reaches) - 1)
+    send_above(0)
+    send_above(1)
 
     image_lane = lax.broadcasted_iota(jnp.int32, (1, cols), 1)
     line = lax.broadcasted_iota(jnp.int32, (LINES, cols), 0)
@@ -487,6 +531,7 @@
     for copy in mate_first:
         copy.wait_send()
     mate_second.wait_send()
+    mate_third.wait_send()
 
     @pl.when(has_far)
     def _():
@@ -543,13 +588,14 @@
             pltpu.VMEM(now.shape, f32),
             pltpu.VMEM((2, *plane), f32),
             pltpu.VMEM(plane, jnp.int32),
-            pltpu.VMEM(now.shape, f32),
+            pltpu.VMEM((2, *plane), f32),
+            pltpu.VMEM((2, *plane), f32),
             pltpu.VMEM((3, 2, *plane), f32),
             pltpu.VMEM((4, 2, *plane), f32),
             pltpu.VMEM((2, *plane), jnp.bfloat16),
             pltpu.VMEM((2, *plane), jnp.bfloat16),
             pltpu.VMEM(now.shape, f32),
-            pltpu.VMEM((8, 2, *plane), f32),
+            pltpu.VMEM((9, 2, *plane), f32),
             pltpu.VMEM((7, 4, *plane), f32),
             pltpu.VMEM(plane, f32),
             pltpu.VMEM((lhs_rows, nrec), f32),
@@ -562,13 +608,15 @@
             pltpu.VMEM((NLAG, per, LINES, cols), f32),
             pltpu.VMEM((NLAG, per, LINES, cols), f32),
             pltpu.VMEM((2 * NLAG, LINES * per, cols), f32),
-            pltpu.SemaphoreType.DMA((4,)),
-            pltpu.SemaphoreType.DMA((4,)),
+            pltpu.SemaphoreType.DMA((5,)),
+            pltpu.SemaphoreType.DMA((5,)),
             pltpu.SemaphoreType.DMA((6,)),
             pltpu.SemaphoreType.DMA((6,)),
             pltpu.SemaphoreType.DMA((2, tiles)),
             pltpu.SemaphoreType.DMA((2, tiles)),
             pltpu.SemaphoreType.DMA((10,)),
+            pltpu.SemaphoreType.REGULAR((1,)),
+            pltpu.SemaphoreType.REGULAR((max(1, tiles.bit_length()),)),
             pltpu.SemaphoreType.REGULAR((max(1, tiles.bit_length()),)),
         ],
         compiler_params=pltpu.CompilerParams(collective_id=0, has_side_effects=True),

time: 18.2 us -> 18 us (0.989)
  Pallas kernels: 16.7 us -> 16.5 us
    pallas_call x1, Pallas kernels: 15.9 us -> 15.7 us  [shards(): pl.pallas_call(functools.partial(kernel, tiles), out_shape=(pltpu.VMEM((N...]
where the time goes in v3:
time: 18 us; the launch traced here: 17.8 us
  Pallas kernels  16.5 us (92%)
  between operations  1.29 us (7%)
    pallas_call x1, Pallas kernels, shards(): pl.pallas_call(functools.partial(kernel, tiles), out_shape=(pltpu.VMEM((N...  15.7 us
    pallas_call x1, Pallas kernels, shards(): pl.pallas_call(stored, out_shape=(jax.ShapeDtypeStruct(filtered.shape, jn...  0.82 us

profile of v3, /device:TPU:0, one launch (start us, length us, event | category | flops | bytes accessed | tf_op | source)
XLA Modules:
  0.0 17.8 jit_solution(12880151455442769289)
XLA Ops:
  1.3 15.7 %shard_map.113 = (bf16[32,4,16,128]{3,2,1,0:T(8,128)(2,1)S(1)}, f32[2,2,32,128]{3,2,1,0:T(8,128)S(1)}) custom-call(f32[2,2,32,128]{3,2,1,0:T(8,128)} %now.1, f32[2,2,32,128]{3,2,1,0:T(8,128)} %prev_in.1, s32[2,32,128]{2,1,0:T(8,128)} %facies_in.1, f32[8]{0:T(128)} %vel_in.1, f32[8]{0:T(128)} %eps_in.1, f32[8]{0:T(128)} %tilt_in.1, s32[1]{0:T(128)S(6)} %copy.12.src_in, ...), custom_call_target="tpu_custom_call" | custom-call | tf_op jit(solution)/shard_map/pallas_call | solution.py:569
  17.0 0.8 %shard_map.114 = (bf16[32,4,16,128]{3,2,1,0:T(8,128)(2,1)}, f32[2,2,32,128]{3,2,1,0:T(8,128)}) custom-call(bf16[32,4,16,128]{3,2,1,0:T(8,128)(2,1)S(1)} %get-tuple-element.6.filtered_in, f32[2,2,32,128]{3,2,1,0:T(8,128)S(1)} %get-tuple-element.7.wave_in), custom_call_target="tpu_custom_call" | custom-call | tf_op jit(solution)/shard_map/pallas_call | solution.py:624

commit v4 on v3

--- a/solution.py
+++ b/solution.py
@@ -308,6 +308,14 @@
             1, f, 0, advance(0, work[3, f], None, work[0, f], own[f, odd])
         )
     to_far(far_second)
+    beyond_next = jnp.minimum(tiles - 2 - me, reach - 1)
+
+    @pl.when(beyond_next > 0)
+    def _():
+        pl.semaphore_wait(entered_sem.at[0], beyond_next)
+
+    if reaches:
+        tell(0)
     for copy in mate_first[1:]:
         copy.wait_recv()
     fill_coef(2, mate_fac[...])
@@ -320,21 +328,13 @@
         trace_send[2, f] = inject(2, f, 0, advance(0, trace_send[1, f], None, near, work[3, f]))
     to_far(far_third)
 
-    beyond_next = jnp.minimum(tiles - 2 - me, reach - 1)
-
-    @pl.when(beyond_next > 0)
-    def _():
-        pl.semaphore_wait(entered_sem.at[0], beyond_next)
-
-    if reaches:
-        tell(0)
-
-    from_far(far_fac)
-    fill_coef(3, fac_recv[0].astype(jnp.float32))
+
     if len(reaches) > 1:
         hear_below(0)
         hear_above(0)
         tell(1)
+    from_far(far_fac)
+    fill_coef(3, fac_recv[0].astype(jnp.float32))
     from_far(far_now)
     for f in range(2):
         push = coef[1, 0] * trace_recv[0, f]

time: 18 us -> 18 us (level)
  no operation moved by 1% of the time
where the time goes in v4:
time: 18 us; the launch traced here: 17.8 us
  Pallas kernels  16.5 us (92%)
  between operations  1.29 us (7%)
    pallas_call x1, Pallas kernels, shards(): pl.pallas_call(functools.partial(kernel, tiles), out_shape=(pltpu.VMEM((N...  15.7 us
    pallas_call x1, Pallas kernels, shards(): pl.pallas_call(stored, out_shape=(jax.ShapeDtypeStruct(filtered.shape, jn...  0.82 us

profile of v4, /device:TPU:0, one launch (start us, length us, event | category | flops | bytes accessed | tf_op | source)
XLA Modules:
  0.0 17.8 jit_solution(2362427915967484662)
XLA Ops:
  1.3 15.7 %shard_map.113 = (bf16[32,4,16,128]{3,2,1,0:T(8,128)(2,1)S(1)}, f32[2,2,32,128]{3,2,1,0:T(8,128)S(1)}) custom-call(f32[2,2,32,128]{3,2,1,0:T(8,128)} %now.1, f32[2,2,32,128]{3,2,1,0:T(8,128)} %prev_in.1, s32[2,32,128]{2,1,0:T(8,128)} %facies_in.1, f32[8]{0:T(128)} %vel_in.1, f32[8]{0:T(128)} %eps_in.1, f32[8]{0:T(128)} %tilt_in.1, s32[1]{0:T(128)S(6)} %copy.12.src_in, ...), custom_call_target="tpu_custom_call" | custom-call | tf_op jit(solution)/shard_map/pallas_call | solution.py:569
  17.0 0.8 %shard_map.114 = (bf16[32,4,16,128]{3,2,1,0:T(8,128)(2,1)}, f32[2,2,32,128]{3,2,1,0:T(8,128)}) custom-call(bf16[32,4,16,128]{3,2,1,0:T(8,128)(2,1)S(1)} %get-tuple-element.6.filtered_in, f32[2,2,32,128]{3,2,1,0:T(8,128)S(1)} %get-tuple-element.7.wave_in), custom_call_target="tpu_custom_call" | custom-call | tf_op jit(solution)/shard_map/pallas_call | solution.py:624
